TPU v7x, 512 devices: a whole 4x4x16 slice. The times are simulated.
512 devices in a mesh: dp: 8 (over y_hi, x), feat: 64 (over y_lo, z, core).
Axes of the slice: x: 4, y: 4 (y_hi: 2, y_lo: 2; y = y_hi * 2 + y_lo), z: 16, core: 2. Of those that a mesh axis runs over, the one named last changes fastest.
Arguments:
- residuals: bfloat16 [384, 2, 8192], P('feat', None, 'dp'), may hold values from -6 to 6
- enc_w: bfloat16 [2, 8192, 16384], P(None, 'dp', 'feat'), may hold values from -0.046875 to 0.046875
- enc_b: float32 [16384], P('feat'), may hold values from 0.5 to 3
- dec_w: bfloat16 [2, 16384, 8192], P(None, 'feat', 'dp'), may hold values from -0.75 to 0.75
- dec_b: float32 [2, 8192], P(None, 'dp'), may hold values from -3 to 3
- active: int32 [384, 64], replicated, may hold values from 0 to 16383, all different within a row
Outputs:
- recon: bfloat16 [384, 2, 8192], P('feat', None, 'dp')
- enc_grad: bfloat16 [2, 8192, 16384], P(None, 'dp', 'feat')
- enc_bias_grad: float32 [16384], P('feat')
- dec_grad: bfloat16 [2, 16384, 8192], P(None, 'feat', 'dp')
- dec_bias_grad: float32 [2, 8192], P(None, 'dp')
Inputs may be any that keep to these rules, and one draw needn't show every extreme that they name: Each row of active names 64 different features, and every feature is named by some row.
All inputs are finite; a program needn't handle non-finite values.
Results may differ from a plain program's by a relative error of at most 0.0062.
Values may be sent and summed in bfloat16 or wider, within the bound.
A program may use at most 64 MiB of HBM per device.

v0:
```python
import math
import jax
import jax.numpy as jnp
from jax import lax
from jax.sharding import PartitionSpec as P


def feature_mask(active, first_feature, feat_dev):
    columns = first_feature + lax.iota(jnp.int32, feat_dev)
    total_rows, top_count = active.shape
    block_rows = math.gcd(total_rows, 64)
    grouped = active.reshape(total_rows // block_rows, block_rows, top_count)

    def one_block(row_group):
        return jnp.any(row_group[:, :, None] == columns[None, None, :], axis=1).astype(jnp.float32)

    return lax.map(one_block, grouped).reshape(total_rows, feat_dev)


def on_device(residuals, enc_w, enc_b, dec_w, dec_b, active):
    n_layers, width_dev, feat_dev = enc_w.shape
    gathered = lax.all_gather(residuals, "feat", axis=0, tiled=True)
    total_rows = gathered.shape[0]
    flat_in = gathered.reshape(total_rows, n_layers * width_dev)
    partial_value = jnp.dot(
        flat_in, enc_w.reshape(n_layers * width_dev, feat_dev), preferred_element_type=jnp.float32
    )
    pre_act = lax.psum(partial_value, "dp") + enc_b
    first_feature = lax.axis_index("feat") * feat_dev
    mask_table = feature_mask(active, first_feature, feat_dev)
    activation = (jnp.maximum(pre_act, 0.0) * mask_table).astype(jnp.bfloat16)
    rows_act = activation
    summed = lax.psum_scatter(
        jnp.einsum("tf,lfd->tld", rows_act, dec_w, preferred_element_type=jnp.float32),
        "feat",
        scatter_dimension=0,
        tiled=True,
    )
    recon_full = summed + dec_b[None]
    recon = recon_full.astype(jnp.bfloat16)
    resid_grad = ((recon_full - residuals.astype(jnp.float32)) * 0.25).astype(jnp.bfloat16)
    dec_bias_grad = lax.psum(jnp.sum(resid_grad.astype(jnp.float32), axis=0), "feat")
    shard_rows = lax.all_gather(resid_grad, "feat", axis=0, tiled=True)
    rows_act = activation
    dec_part = jnp.einsum("tf,tld->lfd", rows_act, shard_rows, preferred_element_type=jnp.float32)
    rows_grad = jnp.einsum("tld,lfd->tf", shard_rows, dec_w, preferred_element_type=jnp.float32)
    act_grad = lax.psum(rows_grad, "dp")
    pre_grad = jnp.where(activation > 0, act_grad, 0.0).astype(jnp.bfloat16)
    enc_bias_grad = jnp.sum(pre_grad.astype(jnp.float32), axis=0)
    enc_full = lax.dot_general(
        flat_in, pre_grad, (((0,), (0,)), ((), ())), preferred_element_type=jnp.float32
    )
    enc_grad = enc_full.reshape(n_layers, width_dev, feat_dev).astype(jnp.bfloat16)
    return (recon, enc_grad, enc_bias_grad, dec_part.astype(jnp.bfloat16), dec_bias_grad)


def solution(mesh):
    return jax.shard_map(
        on_device,
        mesh=mesh,
        in_specs=(
            P("feat", None, "dp"),
            P(None, "dp", "feat"),
            P("feat"),
            P(None, "feat", "dp"),
            P(None, "dp"),
            P(),
        ),
        out_specs=(
            P("feat", None, "dp"),
            P(None, "dp", "feat"),
            P("feat"),
            P(None, "feat", "dp"),
            P(None, "dp"),
        ),
        check_vma=False,
    )
```

profile of v0, /device:TPU:32, one launch (start us, length us, event | category | flops | bytes accessed | tf_op | source)
XLA Modules:
  0.0 868.6 jit_solution(2838763191016575245)
XLA Ops:
  7.2 0.0 copy-start
  7.2 0.0 all-gather.3.cloned.1.call-start
  7.2 0.7 all-gather.3.cloned.1.call-update
  7.9 0.0 all-reduce.5.cloned.1.call-start
  8.0 1.0 copy.33
  9.0 127.1 %all-gather.3.cloned.1.call-done = bf16[384,2,1024]{2,1,0:T(2,128)(2,1)} async-done(((bf16[6,2,1024]{2,1,0:T(2,128)(2,1)}), bf16[384,2,1024]{2,1,0:T(2,128)(2,1)}) %all-gather.3.cloned.1.call-update) | async-done | bytes 1572880 | tf_op jit(solution)/shard_map/all_gather | solution.py:22
  136.1 3.7 copy.36
  139.9 0.0 copy-start.3
  139.9 2.6 convolution_bitcast_fusion
  142.5 0.0 all-reduce.5.cloned.1.call-update
  142.5 0.0 all-reduce.7.cloned.1.call-start
  142.5 4.8 while.11
  142.6 0.7 compare_reduce_fusion.2
  143.4 0.7 compare_reduce_fusion.2
  144.2 0.7 compare_reduce_fusion.2
  144.9 0.7 compare_reduce_fusion.2
  145.7 0.7 compare_reduce_fusion.2
  146.5 0.7 compare_reduce_fusion.2
  147.3 92.5 %all-reduce.5.cloned.1.call-done = f32[384,256]{1,0:T(8,128)} async-done(((f32[384,256]{1,0:T(8,128)}), f32[384,256]{1,0:T(8,128)}) %all-reduce.5.cloned.1.call-update) | async-done | bytes 393232 | tf_op jit(solution)/shard_map/psum | solution.py:28
  239.8 0.0 copy-done.3
  239.8 1.1 fusion.12
  240.8 0.0 copy-done
  240.9 0.6 fusion.14
  241.4 4.1 copy.34
  245.6 0.0 copy-start.1
  245.6 0.0 copy-start.2
  245.6 0.0 all-reduce.7.cloned.1.call-update
  245.6 0.0 all-gather.5.cloned.1.call-start
  245.7 1.3 dynamic-slice
  247.6 439.7 %all-reduce.7.cloned.1.call-done = f32[384,2,1024]{2,1,0:T(2,128)} async-done(((f32[384,2,1024]{2,1,0:T(2,128)}), f32[384,2,1024]{2,1,0:T(2,128)}) %all-reduce.7.cloned.1.call-update) | async-done | bytes 3145744
  687.3 0.0 copy-done.1
  687.3 0.0 copy-done.2
  687.3 1.5 convert_reduce_fusion.1
  688.8 0.0 all-gather.5.cloned.1.call-update
  688.8 108.1 %psum.23 = f32[2,1024]{1,0:T(2,128)} all-reduce(f32[2,1024]{1,0:T(2,128)S(1)} %get-tuple-element.67), channel_id=1, replica_groups=mesh['dp'=8,'feat'=64] {'feat'}, use_global_device_ids=true, to_apply=%region_8.9 | all-reduce | flops 2048 | bytes 16384 | tf_op jit(solution)/shard_map/psum | solution.py:42
  796.9 9.1 %all-gather.5.cloned.1.call-done = bf16[384,2,1024]{2,1,0:T(2,128)(2,1)} async-done(((bf16[6,2,1024]{2,1,0:T(2,128)(2,1)}), bf16[384,2,1024]{2,1,0:T(2,128)(2,1)}) %all-gather.5.cloned.1.call-update) | async-done | bytes 1572880 | tf_op jit(solution)/shard_map/all_gather | solution.py:43
  806.0 2.0 fusion.9
  808.0 45.9 %all-reduce.8 = bf16[384,256]{1,0:T(8,128)(2,1)S(1)} all-reduce(f32[384,256]{1,0:T(8,128)S(1)} %fusion.9), channel_id=1, replica_groups=mesh['dp'=8,'feat'=64] {'dp'}, use_global_device_ids=true, to_apply=%region_5.6 | all-reduce | flops 98304 | bytes 589824 | tf_op jit(solution)/shard_map/psum | solution.py:47
  854.0 0.7 convert_reduce_fusion
  854.6 1.7 fusion.2
  856.3 2.3 copy.40
  858.6 2.2 fusion.6
  860.8 1.3 copy.39
  (19 shorter events, 0.1 us)
Async XLA Ops:
  7.2 233.7 %copy-start = (bf16[2,256,1024]{2,1,0:T(8,128)(2,1)S(1)}, bf16[2,256,1024]{2,1,0:T(8,128)(2,1)}, u32[]{:S(2)}) copy-start(bf16[2,256,1024]{2,1,0:T(8,128)(2,1)} %param.11) | copy-start | bytes 3145732
  7.2 128.9 %all-gather.3.cloned.1.call-start = ((), (), s32[]{:S(2)}) async-start(), calls=%async_computation | async-start | bytes 1597440 | tf_op jit(solution)/shard_map/all_gather | solution.py:22
  7.9 231.9 %all-reduce.5.cloned.1.call-start = ((), (), s32[]{:S(2)}) async-start(), calls=%async_computation.1 | async-start | bytes 786432 | tf_op jit(solution)/shard_map/psum | solution.py:28
  139.9 99.9 %copy-start.3 = (f32[256]{0:T(256)S(1)}, f32[256]{0:T(256)}, u32[]{:S(2)}) copy-start(f32[256]{0:T(256)} %param.10) | copy-start | bytes 3076
  142.5 544.8 %all-reduce.7.cloned.1.call-start = ((), (), s32[]{:S(2)}) async-start(), calls=%async_computation.3 | async-start | bytes 6291456
  245.6 441.7 %copy-start.1 = (bf16[6,2,1024]{2,1,0:T(2,128)(2,1)S(1)}, bf16[6,2,1024]{2,1,0:T(2,128)(2,1)}, u32[]{:S(2)}) copy-start(bf16[6,2,1024]{2,1,0:T(2,128)(2,1)} %param.8) | copy-start | bytes 73732
  245.6 441.7 %copy-start.2 = (f32[2,1024]{1,0:T(2,128)S(1)}, f32[2,1024]{1,0:T(2,128)}, u32[]{:S(2)}) copy-start(f32[2,1024]{1,0:T(2,128)} %param.12) | copy-start | bytes 24580
  245.6 560.4 %all-gather.5.cloned.1.call-start = ((), (), s32[]{:S(2)}) async-start(), calls=%async_computation.2 | async-start | bytes 1597440 | tf_op jit(solution)/shard_map/all_gather | solution.py:43
Sparse Core Ops, SparseCore 0:
  10.1 125.9 all-gather.2
  142.6 97.1 all-reduce.4
  245.7 441.5 all-reduce.6
  689.9 116.0 all-gather.4
where the time goes:
time: 869 us
  waiting for transfers between devices  669 us (77%)
  blocking collectives  154 us (18%)
  between operations  14.5 us (2%)
  local copies, waits for them, and re-layouts  13.8 us (2%)
  matrix products  9.11 us (1%)
    unnamed x5, waiting for transfers between devices  440 us
    all_gather x1, waiting for transfers between devices, on_device(): gathered = lax.all_gather(residuals, 'feat', axis=0, tiled=True)  127 us
    psum x1, blocking collectives, on_device(): lax.psum(jnp.sum(resid_grad.astype(jnp.float32), axis=0), 'feat')  108 us
    psum x1, waiting for transfers between devices, on_device(): pre_act = lax.psum(partial_value, 'dp') + enc_b  92.5 us
    psum x1, blocking collectives, on_device(): act_grad = lax.psum(rows_grad, 'dp')  45.9 us
  transfers between devices with their start and end apart: 4, of which 4 were waited for; matrix products, arithmetic and copies ran while one was open for 1% of the time, Pallas kernels for 0%

commit v1 on v0

--- a/solution.py
+++ b/solution.py
@@ -19,7 +19,9 @@
 
 def on_device(residuals, enc_w, enc_b, dec_w, dec_b, active):
     n_layers, width_dev, feat_dev = enc_w.shape
-    gathered = lax.all_gather(residuals, "feat", axis=0, tiled=True)
+    gathered = jnp.concatenate(
+        lax.all_to_all(jnp.stack([residuals] * lax.axis_size("feat")), "feat", 0, 0), axis=0
+    )
     total_rows = gathered.shape[0]
     flat_in = gathered.reshape(total_rows, n_layers * width_dev)
     partial_value = jnp.dot(

time: 869 us -> 832 us (0.957)
  waiting for transfers between devices: 669 us -> 615 us
  starting transfers between devices: 0.16 us -> 17 us
    all_gather x1 -> x0, waiting for transfers between devices: 127 us -> none  [on_device(): gathered = lax.all_gather(residuals, 'feat', axis=0, tiled=True)]
    all_to_all x0 -> x1, waiting for transfers between devices: none -> 73.9 us  [on_device(): lax.all_to_all(jnp.stack([residuals] * lax.axis_size('feat')), 'feat', 0, 0)]
    all_to_all x0 -> x1, starting transfers between devices: none -> 16.9 us  [on_device(): lax.all_to_all(jnp.stack([residuals] * lax.axis_size('feat')), 'feat', 0, 0)]
    unnamed x5 -> x4, waiting for transfers between devices: 440 us -> 440 us
where the time goes in v1:
time: 832 us
  waiting for transfers between devices  615 us (74%)
  blocking collectives  154 us (19%)
  starting transfers between devices  17 us (2%)
  local copies, waits for them, and re-layouts  15.1 us (2%)
  between operations  14.5 us (2%)
    unnamed x4, waiting for transfers between devices  440 us
    psum x1, blocking collectives, on_device(): lax.psum(jnp.sum(resid_grad.astype(jnp.float32), axis=0), 'feat')  108 us
    psum x1, waiting for transfers between devices, on_device(): pre_act = lax.psum(partial_value, 'dp') + enc_b  92.5 us
    all_to_all x1, waiting for transfers between devices, on_device(): lax.all_to_all(jnp.stack([residuals] * lax.axis_size('feat')), 'feat', 0, 0)  73.9 us
    psum x1, blocking collectives, on_device(): act_grad = lax.psum(rows_grad, 'dp')  45.9 us
    all_to_all x1, starting transfers between devices, on_device(): lax.all_to_all(jnp.stack([residuals] * lax.axis_size('feat')), 'feat', 0, 0)  16.9 us
  transfers between devices with their start and end apart: 4, of which 4 were waited for; matrix products, arithmetic and copies ran while one was open for 1% of the time, Pallas kernels for 0%

profile of v1, /device:TPU:32, one launch (start us, length us, event | category | flops | bytes accessed | tf_op | source)
XLA Modules:
  0.0 831.8 jit_solution(13902866873323948643)
XLA Ops:
  7.2 0.0 copy-start
  7.2 2.8 stack.2
  10.0 0.0 copy-start.2
  10.0 16.9 %all-to-all-start = ((bf16[64,6,2,1024]{3,2,1,0:T(2,128)(2,1)}), bf16[64,6,2,1024]{3,2,1,0:T(2,128)(2,1)S(1)}, u32[]{:S(2)}, u32[]{:S(2)}) async-start(bf16[64,6,2,1024]{3,2,1,0:T(2,128)(2,1)} %stack.2), calls=%async_computation | async-start | bytes 3145728 | tf_op jit(solution)/shard_map/all_to_all | solution.py:23
  26.9 0.0 all-reduce.5.cloned.1.call-start
  26.9 0.0 copy-done.2
  27.0 0.1 copy.22
  27.1 73.9 %all-to-all-done = bf16[64,6,2,1024]{3,2,1,0:T(2,128)(2,1)S(1)} async-done(((bf16[64,6,2,1024]{3,2,1,0:T(2,128)(2,1)}), bf16[64,6,2,1024]{3,2,1,0:T(2,128)(2,1)S(1)}, u32[]{:S(2)}, u32[]{:S(2)}) %all-to-all-start) | async-done | bytes 1572896 | tf_op jit(solution)/shard_map/all_to_all | solution.py:23
  101.0 0.0 copy-start.1
  101.0 1.2 copy-done.1
  102.2 0.0 copy-start.6
  102.2 1.9 copy.29
  104.1 0.0 copy-done.6
  104.1 0.0 copy-start.5
  104.1 1.3 fusion.17
  105.5 0.0 all-reduce.5.cloned.1.call-update
  105.5 0.0 all-reduce.7.cloned.1.call-start
  105.5 4.8 while.11
  105.6 0.7 compare_reduce_fusion.2
  106.4 0.7 compare_reduce_fusion.2
  107.2 0.7 compare_reduce_fusion.2
  107.9 0.7 compare_reduce_fusion.2
  108.7 0.7 compare_reduce_fusion.2
  109.5 0.7 compare_reduce_fusion.2
  110.3 92.5 %all-reduce.5.cloned.1.call-done = f32[384,256]{1,0:T(8,128)} async-done(((f32[384,256]{1,0:T(8,128)}), f32[384,256]{1,0:T(8,128)}) %all-reduce.5.cloned.1.call-update) | async-done | bytes 393232 | tf_op jit(solution)/shard_map/psum | solution.py:30
  202.8 0.0 copy-done.5
  202.8 1.1 fusion.12
  203.8 0.0 copy-done
  203.9 0.6 fusion.14
  204.4 4.1 copy.23
  208.6 0.0 copy-start.3
  208.6 0.0 all-reduce.7.cloned.1.call-update
  208.6 0.0 all-gather.2.cloned.1.call-start
  208.6 1.3 dynamic-slice
  210.6 439.7 %all-reduce.7.cloned.1.call-done = f32[384,2,1024]{2,1,0:T(2,128)} async-done(((f32[384,2,1024]{2,1,0:T(2,128)}), f32[384,2,1024]{2,1,0:T(2,128)}) %all-reduce.7.cloned.1.call-update) | async-done | bytes 3145744
  650.3 0.0 copy-done.3
  650.3 0.0 copy-done.4
  650.3 1.5 convert_reduce_fusion.1
  651.8 0.0 all-gather.2.cloned.1.call-update
  651.8 108.2 %psum.23 = f32[2,1024]{1,0:T(2,128)} all-reduce(f32[2,1024]{1,0:T(2,128)S(1)} %get-tuple-element.62), channel_id=1, replica_groups=mesh['dp'=8,'feat'=64] {'feat'}, use_global_device_ids=true, to_apply=%region_8.9 | all-reduce | flops 2048 | bytes 16384 | tf_op jit(solution)/shard_map/psum | solution.py:44
  760.0 9.2 %all-gather.2.cloned.1.call-done = bf16[384,2,1024]{2,1,0:T(2,128)(2,1)} async-done(((bf16[6,2,1024]{2,1,0:T(2,128)(2,1)}), bf16[384,2,1024]{2,1,0:T(2,128)(2,1)}) %all-gather.2.cloned.1.call-update) | async-done | bytes 1572880 | tf_op jit(solution)/shard_map/all_gather | solution.py:45
  769.2 2.0 fusion.9
  771.2 45.9 %all-reduce.8 = bf16[384,256]{1,0:T(8,128)(2,1)S(1)} all-reduce(f32[384,256]{1,0:T(8,128)S(1)} %fusion.9), channel_id=1, replica_groups=mesh['dp'=8,'feat'=64] {'dp'}, use_global_device_ids=true, to_apply=%region_5.6 | all-reduce | flops 98304 | bytes 589824 | tf_op jit(solution)/shard_map/psum | solution.py:49
  817.1 1.7 fusion.2
  818.8 0.7 convert_reduce_fusion
  819.5 2.3 copy.28
  821.7 2.2 fusion.6
  823.9 1.3 copy.27
  (20 shorter events, 0.1 us)
Async XLA Ops:
  7.2 196.7 %copy-start = (bf16[2,256,1024]{2,1,0:T(8,128)(2,1)S(1)}, bf16[2,256,1024]{2,1,0:T(8,128)(2,1)}, u32[]{:S(2)}) copy-start(bf16[2,256,1024]{2,1,0:T(8,128)(2,1)} %param.11) | copy-start | bytes 3145732
  10.0 17.0 %copy-start.2 = (s32[384,64]{0,1:T(8,128)S(1)}, s32[384,64]{0,1:T(8,128)}, u32[]{:S(2)}) copy-start(s32[384,64]{0,1:T(8,128)} %param.13) | copy-start | bytes 294916
  10.0 91.0 %all-to-all-start = ((bf16[64,6,2,1024]{3,2,1,0:T(2,128)(2,1)}), bf16[64,6,2,1024]{3,2,1,0:T(2,128)(2,1)S(1)}, u32[]{:S(2)}, u32[]{:S(2)}) async-start(bf16[64,6,2,1024]{3,2,1,0:T(2,128)(2,1)} %stack.2), calls=%async_computation | async-start | bytes 3145728 | tf_op jit(solution)/shard_map/all_to_all | solution.py:23
  26.9 175.9 %all-reduce.5.cloned.1.call-start = ((), (), s32[]{:S(2)}) async-start(), calls=%async_computation.1 | async-start | bytes 786432 | tf_op jit(solution)/shard_map/psum | solution.py:30
  101.0 1.2 copy-start.1
  102.2 1.9 copy-start.6
  104.1 98.7 %copy-start.5 = (f32[256]{0:T(256)S(1)}, f32[256]{0:T(256)}, u32[]{:S(2)}) copy-start(f32[256]{0:T(256)} %param.10) | copy-start | bytes 3076
  105.5 544.8 %all-reduce.7.cloned.1.call-start = ((), (), s32[]{:S(2)}) async-start(), calls=%async_computation.3 | async-start | bytes 6291456
  208.6 441.7 %copy-start.3 = (bf16[6,2,1024]{2,1,0:T(2,128)(2,1)S(1)}, bf16[6,2,1024]{2,1,0:T(2,128)(2,1)}, u32[]{:S(2)}) copy-start(bf16[6,2,1024]{2,1,0:T(2,128)(2,1)} %param.8) | copy-start | bytes 73732
  208.6 441.7 %copy-start.4 = (f32[2,1024]{1,0:T(2,128)S(1)}, f32[2,1024]{1,0:T(2,128)}, u32[]{:S(2)}) copy-start(f32[2,1024]{1,0:T(2,128)} %param.12) | copy-start | bytes 24580
  208.6 560.6 %all-gather.2.cloned.1.call-start = ((), (), s32[]{:S(2)}) async-start(), calls=%async_computation.2 | async-start | bytes 1597440 | tf_op jit(solution)/shard_map/all_gather | solution.py:45
Sparse Core Ops, SparseCore 0:
  105.6 97.1 all-reduce.4
  208.7 441.5 all-reduce.6
  653.0 116.1 all-gather.1
